TPU v7x, 32 devices: a whole 2x2x4 slice. The times are simulated.
32 devices in a mesh: group: 2 (over y), row: 4 (over z), col: 2 (over x), sub: 2 (over core).
Axes of the slice: x: 2, y: 2, z: 4, core: 2. Of those that a mesh axis runs over, the one named last changes fastest.
Arguments:
- anomalies: bfloat16 [2048, 2048], P(('group', 'row', 'sub')), parts along dimension 0, may hold values from -6 to 6
- innovations: float32 [4096], P(('group', 'row', 'col', 'sub')), parts along dimension 0, may hold values from -12 to 12
- obs_error: float32 [4096], P(('group', 'row', 'col', 'sub')), parts along dimension 0, may hold values from 0.5 to 2
- track_pos: float32 [4096], P('group'), parts along dimension 0, may hold values from 0 to 1
- taper_class: int32 [8, 4], P('group'), parts along dimension 0, may hold values from 0 to 3, as said below
Outputs:
- solution: float32 [4096], P(('group', 'row', 'col', 'sub')), parts along dimension 0
- residual: float32 [4096], P(('group', 'row', 'col', 'sub')), parts along dimension 0
There are 2 independent parts, one for each index of `group`. A program takes and returns all parts, laid end to end along the dimension named above; each array names one. Nothing has to cross between parts.
Inputs may be any that keep to these rules, and one draw needn't show every extreme that they name: `taper_class`: tiles are spatial blocks of the region, laid along the plume in an order given by a permutation pos of the 4 tiles; entry (a, b) is the distance |pos[a] - pos[b]| in tiles.
All inputs are finite; a program needn't handle non-finite values.
Results may differ from a plain program's by a relative error of at most 0.0003.
Values may be sent and summed in bfloat16 or wider, within the bound.
No kernel may reach another device: no remote copies, remote signals or barrier semaphores. Data moves between devices by JAX's collectives and lax.ppermute only.
A program may use at most 64 MiB of HBM per device.

v0:
```python
import jax
import jax.numpy as jnp
from jax import lax
from jax.sharding import PartitionSpec as P

ITERS = 2
track_width = 0.0001


def squares(residual):
    return lax.psum(jnp.sum(residual * residual), ("row", "col", "sub"))


def per_device(anomalies, innovations, obs_error, track_pos, taper_class):
    row_count = lax.axis_size("row")
    col_count = lax.axis_size("col")
    sub_count = lax.axis_size("sub")
    row_index = lax.axis_index("row")
    col_index = lax.axis_index("col")
    local_members, total_obs = anomalies.shape
    block_len = total_obs // row_count
    quarter_len = block_len // col_count
    member_total = local_members * row_count * sub_count
    inverse_members = 1.0 / (member_total - 1)
    reach_tiles = max(2, row_count // 4)
    class_row = lax.dynamic_index_in_dim(taper_class, row_index, 0, keepdims=False)
    tile_weight = jnp.maximum(0.0, 1.0 - class_row.astype(jnp.float32) / reach_tiles)
    row_pos = lax.dynamic_slice_in_dim(track_pos, row_index * block_len, block_len, 0)
    col_pos = lax.dynamic_index_in_dim(
        track_pos.reshape(row_count, col_count, quarter_len), col_index, 1, keepdims=False
    )
    own_block = lax.all_to_all(anomalies, "row", split_axis=1, concat_axis=0, tiled=True)
    own_quarter = lax.dynamic_slice_in_dim(own_block, col_index * quarter_len, quarter_len, 1)

    def one_tile(piece, block_index, keep_factor):
        product = jnp.einsum("mi,mq->iq", own_block, piece, preferred_element_type=jnp.float32)
        column_pos = lax.dynamic_index_in_dim(col_pos, block_index, 0, keepdims=False)
        weight_here = lax.dynamic_index_in_dim(tile_weight, block_index, 0, keepdims=False)
        distance = row_pos[:, None] - column_pos[None, :]
        taper = weight_here * keep_factor * jnp.exp(-(distance * distance) / track_width)
        return product * (taper * inverse_members)

    def one_entry(entry):
        return one_tile(entry[0], entry[1], 1.0)

    piece = lax.all_gather(own_quarter[None], "row", axis=0, tiled=True)
    indices = jnp.arange(piece.shape[0], dtype=jnp.int32)
    tiles = lax.map(one_entry, (piece, indices))
    solution = jnp.zeros_like(innovations)
    residual = innovations
    direction_vec = innovations
    norm_now = squares(residual)
    for turn_index in range(ITERS):
        column_vec = lax.all_gather(direction_vec, ("row", "sub"), axis=0, tiled=True).reshape(
            row_count, quarter_len
        )
        direct = jnp.einsum("jiq,jq->i", tiles, column_vec, precision=lax.Precision.HIGHEST)
        extra = obs_error * direction_vec
        own_part = lax.psum_scatter(direct, ("col", "sub"), scatter_dimension=0, tiled=True)
        image = own_part + extra
        alpha = norm_now / lax.psum(jnp.sum(direction_vec * image), ("row", "col", "sub"))
        solution = solution + alpha * direction_vec
        residual = residual - alpha * image
        if turn_index + 1 < ITERS:
            norm_next = squares(residual)
            direction_vec = residual + norm_next / norm_now * direction_vec
            norm_now = norm_next
    return (solution, residual)


def solution(mesh):
    in_specs = (
        P(("group", "row", "sub"), None),
        P(("group", "row", "col", "sub")),
        P(("group", "row", "col", "sub")),
        P("group"),
        P("group", None),
    )
    out_specs = (P(("group", "row", "col", "sub")), P(("group", "row", "col", "sub")))
    return jax.shard_map(
        per_device, mesh=mesh, in_specs=in_specs, out_specs=out_specs, check_vma=False
    )
```

profile of v0, /device:TPU:0, one launch (start us, length us, event | category | flops | bytes accessed | tf_op | source)
XLA Modules:
  0.0 207.6 jit_solution(16276653144272945120)
XLA Ops:
  7.2 0.0 copy-start.3
  7.2 0.0 copy-start
  7.2 0.0 copy-start.1
  7.2 1.9 copy.16
  9.1 6.3 %all-to-all-start = ((bf16[128,4,512]{2,0,1:T(8,128)(2,1)}), bf16[128,4,512]{2,0,1:T(8,128)(2,1)S(1)}, u32[]{:S(2)}, u32[]{:S(2)}) async-start(bf16[128,4,512]{2,0,1:T(8,128)(2,1)} %bitcast.41), calls=%async_computation | async-start | bytes 1048576 | tf_op jit(solution)/shard_map/all_to_all | solution.py:32
  15.4 0.0 all-gather.5.cloned.1.call-start
  15.4 14.5 %all-to-all-done = bf16[128,4,512]{2,0,1:T(8,128)(2,1)S(1)} async-done(((bf16[128,4,512]{2,0,1:T(8,128)(2,1)}), bf16[128,4,512]{2,0,1:T(8,128)(2,1)S(1)}, u32[]{:S(2)}, u32[]{:S(2)}) %all-to-all-start) | async-done | bytes 524320 | tf_op jit(solution)/shard_map/all_to_all | solution.py:32
  29.9 0.7 constant_dynamic-slice_fusion.3
  30.6 0.0 all-gather.5.cloned.1.call-update
  30.7 0.0 copy-done
  30.7 0.1 dynamic_slice.32
  30.8 0.0 copy-done.3
  30.8 0.6 dynamic-slice
  32.0 0.0 copy-done.1
  32.1 9.8 %all-gather.1 = f32[8,1,128]{2,1,0:T(1,128)S(1)} all-gather(f32[1,1,128]{2,1,0:T(1,128)S(1)} %bitcast.64), channel_id=1, replica_groups=mesh['group'=2,'row'=4,'col'=2,'sub'=2] {'row','sub'}, dimensions={0}, use_global_device_ids=true | all-gather | bytes 4608 | tf_op jit(solution)/shard_map/all_gather | solution.py:54
  41.8 0.7 maximum_bitcast_fusion
  42.5 15.3 %all-gather.5.cloned.1.call-done = bf16[2048,256]{1,0:T(8,128)(2,1)} async-done(((bf16[512,256]{1,0:T(8,128)(2,1)}), bf16[2048,256]{1,0:T(8,128)(2,1)}) %all-gather.5.cloned.1.call-update) | async-done | bytes 1048592 | tf_op jit(solution)/shard_map/all_gather | solution.py:46
  57.8 20.4 %while.10 = (s32[]{:T(128)}, f32[4,512,256]{1,2,0:T(8,128)S(1)}, bf16[4,512,256]{2,1,0:T(8,128)(2,1)}, bf16[512,512]{1,0:T(8,128)(2,1)S(1)}, s32[4]{0:T(128)S(1)...) while((s32[]{:T(128)}, f32[4,512,256]{1,2,0:T(8,128)S(1)}, ...), condition=%wide.region_3.4_spmd, body=%wide.region_2.3_spmd.sunk | while | flops 135135232 | bytes 1317547 | solution.py:48
  57.8 0.6 dynamic_slice.56
  60.4 0.6 dynamic_slice.57
  61.0 1.9 fusion.21
  62.9 0.6 dynamic_slice.56
  65.5 0.6 dynamic_slice.57
  66.1 1.9 fusion.21
  68.0 0.6 dynamic_slice.56
  70.6 0.6 dynamic_slice.57
  71.2 1.9 fusion.21
  73.1 0.6 dynamic_slice.56
  75.7 0.6 dynamic_slice.57
  76.3 1.9 fusion.21
  78.2 0.0 copy-start.2
  78.2 1.2 fusion.9
  79.4 6.4 %all-reduce = f32[512]{0:T(512)S(1)} all-reduce(f32[512]{0:T(512)S(1)} %bitcast.66), channel_id=3, replica_groups=mesh['group'=2,'row'=4,'col'=2,'sub'=2] {'col','sub'}, use_global_device_ids=true, to_apply=%region_4.5.clone | all-reduce | flops 512 | bytes 4096
  85.8 0.0 copy-done.2
  85.8 0.7 multiply_reduce_fusion.2
  86.5 31.6 %all-reduce.2 = (f32[]{:T(128)}, f32[]{:T(128)}) all-reduce(f32[]{:T(128)} %get-tuple-element.46, f32[]{:T(128)} %get-tuple-element.45), channel_id=1, replica_groups=mesh['group'=2,'row'=4,'col'=2,'sub'=2] {'row','col','sub'}, use_global_device_ids=true, to_apply=%region_1.2 | all-reduce | flops 2 | bytes 16 | tf_op jit(solution)/shard_map/psum | solution.py:11
  119.5 0.7 multiply_reduce_fusion.1
  120.1 30.1 %psum.30 = f32[]{:T(128)} all-reduce(f32[]{:T(128)} %get-tuple-element.65), channel_id=1, replica_groups=mesh['group'=2,'row'=4,'col'=2,'sub'=2] {'row','col','sub'}, use_global_device_ids=true, to_apply=%region_8.9 | all-reduce | flops 1 | bytes 8 | tf_op jit(solution)/shard_map/psum | solution.py:11
  151.6 8.4 %all-gather.2 = f32[8,1,128]{2,1,0:T(1,128)S(1)} all-gather(f32[1,1,128]{2,1,0:T(1,128)S(1)} %bitcast.67), channel_id=1, replica_groups=mesh['group'=2,'row'=4,'col'=2,'sub'=2] {'row','sub'}, dimensions={0}, use_global_device_ids=true | all-gather | bytes 4608 | tf_op jit(solution)/shard_map/all_gather | solution.py:54
  160.0 1.2 fusion.10
  161.2 5.9 %all-reduce.1 = f32[512]{0:T(512)S(1)} all-reduce(f32[512]{0:T(512)S(1)} %bitcast.65), channel_id=4, replica_groups=mesh['group'=2,'row'=4,'col'=2,'sub'=2] {'col','sub'}, use_global_device_ids=true, to_apply=%region_9.10.clone | all-reduce | flops 512 | bytes 4096
  167.1 0.7 multiply_reduce_fusion
  167.8 31.1 %psum.31 = f32[]{:T(128)} all-reduce(f32[]{:T(128)} %multiply_reduce_fusion), channel_id=1, replica_groups=mesh['group'=2,'row'=4,'col'=2,'sub'=2] {'row','col','sub'}, use_global_device_ids=true, to_apply=%region_11.12 | all-reduce | flops 1 | bytes 8 | tf_op jit(solution)/shard_map/psum | solution.py:61
  200.2 0.6 multiply_subtract_fusion
  (10 shorter events, 0.1 us)
Async XLA Ops:
  7.2 23.6 %copy-start.3 = (u32[32]{0:T(128)S(1)}, u32[32]{0:T(128)}, u32[]{:S(2)}) copy-start(u32[32]{0:T(128)} %constant.61) | copy-start | bytes 388
  7.2 23.5 %copy-start = (f32[2048]{0:T(1024)S(1)}, f32[2048]{0:T(1024)}, u32[]{:S(2)}) copy-start(f32[2048]{0:T(1024)} %param.10) | copy-start | bytes 24580
  7.2 24.9 %copy-start.1 = (f32[128]{0:T(128)S(1)}, f32[128]{0:T(128)}, u32[]{:S(2)}) copy-start(f32[128]{0:T(128)} %param.8) | copy-start | bytes 1540
  9.1 20.8 %all-to-all-start = ((bf16[128,4,512]{2,0,1:T(8,128)(2,1)}), bf16[128,4,512]{2,0,1:T(8,128)(2,1)S(1)}, u32[]{:S(2)}, u32[]{:S(2)}) async-start(bf16[128,4,512]{2,0,1:T(8,128)(2,1)} %bitcast.41), calls=%async_computation | async-start | bytes 1048576 | tf_op jit(solution)/shard_map/all_to_all | solution.py:32
  15.4 42.4 %all-gather.5.cloned.1.call-start = ((), (), s32[]{:S(2)}) async-start(), calls=%async_computation.1 | async-start | bytes 1310720 | tf_op jit(solution)/shard_map/all_gather | solution.py:46
  78.2 7.6 %copy-start.2 = (f32[128]{0:T(128)S(1)}, f32[128]{0:T(128)}, u32[]{:S(2)}) copy-start(f32[128]{0:T(128)} %param.9) | copy-start | bytes 1540
Sparse Core Ops, SparseCore 0:
  30.8 27.0 all-gather.4
where the time goes:
time: 208 us
  blocking collectives  123 us (59%)
  waiting for transfers between devices  29.8 us (14%)
  between operations  18.8 us (9%)
  matrix products  10.1 us (5%)
  local copies, waits for them, and re-layouts  8.07 us (4%)
  loops' own time  7.89 us (4%)
  starting transfers between devices  6.32 us (3%)
  other arithmetic  3.32 us (2%)
    psum x2, blocking collectives, squares(): return lax.psum(jnp.sum(residual * residual), ('row', 'col', 'sub'))  61.7 us
    psum x1, blocking collectives, per_device(): lax.psum(jnp.sum(direction_vec * image), ('row', 'col', 'sub'))  31.1 us
    all_gather x2, blocking collectives, per_device(): lax.all_gather(direction_vec, ('row', 'sub'), axis=0, tiled=True)  18.2 us
    all_gather x1, waiting for transfers between devices, per_device(): piece = lax.all_gather(own_quarter[None], 'row', axis=0, tiled=True)  15.3 us
    all_to_all x1, waiting for transfers between devices, per_device(): lax.all_to_all(anomalies, 'row', split_axis=1, concat_axis=0, tiled=True)  14.5 us
    unnamed x2, blocking collectives  12.3 us
    another operation x1, loops' own time, per_device(): tiles = lax.map(one_entry, (piece, indices))  7.89 us
    dot_general x4, matrix products, one_tile(): jnp.einsum('mi,mq->iq', own_block, piece, preferred_element_type=jnp.floa...  7.74 us
  transfers between devices with their start and end apart: 2, of which 2 were waited for; matrix products, arithmetic and copies ran while one was open for 1% of the time, Pallas kernels for 0%

commit v1 on v0

--- a/solution.py
+++ b/solution.py
@@ -43,7 +43,12 @@
     def one_entry(entry):
         return one_tile(entry[0], entry[1], 1.0)
 
-    piece = lax.all_gather(own_quarter[None], "row", axis=0, tiled=True)
+    ring = [own_quarter[None]]
+    for hop in range(3):
+        ring.append(lax.ppermute(ring[-1], "row", [(dev, (dev + 1) % 4) for dev in range(4)]))
+    piece = jnp.roll(
+        jnp.concatenate(ring[::-1], axis=0), (lax.axis_index("row") + 1) * ring[0].shape[0], axis=0
+    )
     indices = jnp.arange(piece.shape[0], dtype=jnp.int32)
     tiles = lax.map(one_entry, (piece, indices))
     solution = jnp.zeros_like(innovations)

time: 208 us -> 199 us (0.957)
  between operations: 18.8 us -> 5.46 us
    ppermute x0 -> x3, waiting for transfers between devices: none -> 17.2 us  [per_device(): lax.ppermute(ring[-1], 'row', [(dev, (dev + 1) % 4) for dev in range(4)])]
    all_gather x1 -> x0, waiting for transfers between devices: 15.3 us -> none  [per_device(): piece = lax.all_gather(own_quarter[None], 'row', axis=0, tiled=True)]
    all_gather x2, blocking collectives: 18.2 us -> 20.5 us  [per_device(): lax.all_gather(direction_vec, ('row', 'sub'), axis=0, tiled=True)]
  transfers between devices with their start and end apart: 2 -> 4, of which waited for: 2 -> 3; matrix products, arithmetic and copies ran while one was open for 1% -> 1% of each run, Pallas kernels for 0% -> 0%
where the time goes in v1:
time: 199 us; the launch traced here: 198 us
  blocking collectives  125 us (63%)
  waiting for transfers between devices  31.7 us (16%)
  matrix products  10.1 us (5%)
  local copies, waits for them, and re-layouts  8.57 us (4%)
  loops' own time  7.89 us (4%)
  starting transfers between devices  6.38 us (3%)
  between operations  5.46 us (3%)
  other arithmetic  3.32 us (2%)
    psum x2, blocking collectives, squares(): return lax.psum(jnp.sum(residual * residual), ('row', 'col', 'sub'))  60.2 us
    psum x1, blocking collectives, per_device(): lax.psum(jnp.sum(direction_vec * image), ('row', 'col', 'sub'))  31.1 us
    all_gather x2, blocking collectives, per_device(): lax.all_gather(direction_vec, ('row', 'sub'), axis=0, tiled=True)  20.5 us
    ppermute x3, waiting for transfers between devices, per_device(): lax.ppermute(ring[-1], 'row', [(dev, (dev + 1) % 4) for dev in range(4)])  17.2 us
    all_to_all x1, waiting for transfers between devices, per_device(): lax.all_to_all(anomalies, 'row', split_axis=1, concat_axis=0, tiled=True)  14.5 us
    unnamed x2, blocking collectives  13 us
    another operation x1, loops' own time, per_device(): tiles = lax.map(one_entry, (piece, indices))  7.89 us
    dot_general x4, matrix products, one_tile(): jnp.einsum('mi,mq->iq', own_block, piece, preferred_element_type=jnp.floa...  7.75 us
  transfers between devices with their start and end apart: 4, of which 3 were waited for; matrix products, arithmetic and copies ran while one was open for 1% of the time, Pallas kernels for 0%

profile of v1, /device:TPU:0, one launch (start us, length us, event | category | flops | bytes accessed | tf_op | source)
XLA Modules:
  0.0 198.3 jit_solution(7910213217760824774)
XLA Ops:
  0.6 0.0 copy-start.3
  0.6 0.0 copy-start
  0.7 0.0 copy-start.1
  0.7 1.9 copy.16
  2.5 6.3 %all-to-all-start = ((bf16[128,4,512]{2,0,1:T(8,128)(2,1)}), bf16[128,4,512]{2,0,1:T(8,128)(2,1)S(1)}, u32[]{:S(2)}, u32[]{:S(2)}) async-start(bf16[128,4,512]{2,0,1:T(8,128)(2,1)} %bitcast.46), calls=%async_computation | async-start | bytes 1048576 | tf_op jit(solution)/shard_map/all_to_all | solution.py:32
  8.9 14.5 %all-to-all-done = bf16[128,4,512]{2,0,1:T(8,128)(2,1)S(1)} async-done(((bf16[128,4,512]{2,0,1:T(8,128)(2,1)}), bf16[128,4,512]{2,0,1:T(8,128)(2,1)S(1)}, u32[]{:S(2)}, u32[]{:S(2)}) %all-to-all-start) | async-done | bytes 524320 | tf_op jit(solution)/shard_map/all_to_all | solution.py:32
  23.4 0.1 collective-permute-start
  23.4 9.1 %collective-permute-done = bf16[1,512,256]{2,1,0:T(8,128)(2,1)S(1)} collective-permute-done((bf16[1,512,256]{2,1,0:T(8,128)(2,1)S(1)}, bf16[1,512,256]{2,1,0:T(8,128)(2,1)S(1)}, u32[]{:S(2)}, u32[]{:S(2)}) %collective-permute-start) | collective-permute-done | bytes 262176 | tf_op jit(solution)/shard_map/ppermute | solution.py:48
  32.5 0.0 collective-permute-start.1
  32.5 8.2 %collective-permute-done.1 = bf16[1,512,256]{2,1,0:T(8,128)(2,1)S(1)} collective-permute-done((bf16[1,512,256]{2,1,0:T(8,128)(2,1)S(1)}, bf16[1,512,256]{2,1,0:T(8,128)(2,1)S(1)}, u32[]{:S(2)}, u32[]{:S(2)}) %collective-permute-start.1) | collective-permute-done | bytes 262176 | tf_op jit(solution)/shard_map/ppermute | solution.py:48
  40.7 0.0 collective-permute-start.2
  40.7 0.0 copy-done
  40.7 0.1 dynamic_slice.37
  40.8 0.0 copy-done.3
  40.8 0.6 dynamic-slice
  42.0 0.0 copy-done.1
  42.1 12.2 %all-gather = f32[8,1,128]{2,1,0:T(1,128)S(1)} all-gather(f32[1,1,128]{2,1,0:T(1,128)S(1)} %bitcast.71), channel_id=1, replica_groups=mesh['group'=2,'row'=4,'col'=2,'sub'=2] {'row','sub'}, dimensions={0}, use_global_device_ids=true | all-gather | bytes 4608 | tf_op jit(solution)/shard_map/all_gather | solution.py:59
  54.2 0.7 maximum_bitcast_fusion
  54.9 0.0 collective-permute-done.2
  55.1 1.1 constant_dynamic-slice_fusion.3
  56.2 20.4 %while.10 = (s32[]{:T(128)}, f32[4,512,256]{1,2,0:T(8,128)S(1)}, bf16[4,512,256]{2,1,0:T(8,128)(2,1)}, bf16[512,512]{1,0:T(8,128)(2,1)S(1)}, s32[4]{0:T(128)S(1)...) while((s32[]{:T(128)}, f32[4,512,256]{1,2,0:T(8,128)S(1)}, ...), condition=%wide.region_3.4_spmd, body=%wide.region_2.3_spmd.sunk | while | flops 135135232 | bytes 1317547 | solution.py:53
  56.2 0.6 dynamic_slice.66
  58.7 0.6 dynamic_slice.67
  59.3 1.9 fusion.21
  61.3 0.6 dynamic_slice.66
  63.8 0.6 dynamic_slice.67
  64.4 1.9 fusion.21
  66.4 0.6 dynamic_slice.66
  68.9 0.6 dynamic_slice.67
  69.5 1.9 fusion.21
  71.5 0.6 dynamic_slice.66
  74.0 0.6 dynamic_slice.67
  74.6 1.9 fusion.21
  76.6 0.0 copy-start.2
  76.6 1.2 fusion.9
  77.8 7.0 %all-reduce = f32[512]{0:T(512)S(1)} all-reduce(f32[512]{0:T(512)S(1)} %bitcast.73), channel_id=2, replica_groups=mesh['group'=2,'row'=4,'col'=2,'sub'=2] {'col','sub'}, use_global_device_ids=true, to_apply=%region_4.5.clone | all-reduce | flops 512 | bytes 4096
  84.8 0.0 copy-done.2
  84.8 0.7 multiply_reduce_fusion.2
  85.5 30.1 %all-reduce.2 = (f32[]{:T(128)}, f32[]{:T(128)}) all-reduce(f32[]{:T(128)} %get-tuple-element.46, f32[]{:T(128)} %get-tuple-element.45), channel_id=1, replica_groups=mesh['group'=2,'row'=4,'col'=2,'sub'=2] {'row','col','sub'}, use_global_device_ids=true, to_apply=%region_1.2 | all-reduce | flops 2 | bytes 16 | tf_op jit(solution)/shard_map/psum | solution.py:11
  116.9 0.7 multiply_reduce_fusion.1
  117.6 30.1 %psum.30 = f32[]{:T(128)} all-reduce(f32[]{:T(128)} %get-tuple-element.65), channel_id=1, replica_groups=mesh['group'=2,'row'=4,'col'=2,'sub'=2] {'row','col','sub'}, use_global_device_ids=true, to_apply=%region_8.9 | all-reduce | flops 1 | bytes 8 | tf_op jit(solution)/shard_map/psum | solution.py:11
  149.1 8.4 %all-gather.1 = f32[8,1,128]{2,1,0:T(1,128)S(1)} all-gather(f32[1,1,128]{2,1,0:T(1,128)S(1)} %bitcast.74), channel_id=1, replica_groups=mesh['group'=2,'row'=4,'col'=2,'sub'=2] {'row','sub'}, dimensions={0}, use_global_device_ids=true | all-gather | bytes 4608 | tf_op jit(solution)/shard_map/all_gather | solution.py:59
  157.4 1.2 fusion.10
  158.6 5.9 %all-reduce.1 = f32[512]{0:T(512)S(1)} all-reduce(f32[512]{0:T(512)S(1)} %bitcast.72), channel_id=3, replica_groups=mesh['group'=2,'row'=4,'col'=2,'sub'=2] {'col','sub'}, use_global_device_ids=true, to_apply=%region_9.10.clone | all-reduce | flops 512 | bytes 4096
  164.6 0.7 multiply_reduce_fusion
  165.2 31.1 %psum.31 = f32[]{:T(128)} all-reduce(f32[]{:T(128)} %multiply_reduce_fusion), channel_id=1, replica_groups=mesh['group'=2,'row'=4,'col'=2,'sub'=2] {'row','col','sub'}, use_global_device_ids=true, to_apply=%region_11.12 | all-reduce | flops 1 | bytes 8 | tf_op jit(solution)/shard_map/psum | solution.py:66
  197.7 0.6 multiply_subtract_fusion
  (19 shorter events, 0.2 us)
Async XLA Ops:
  0.6 40.2 %copy-start.3 = (u32[32]{0:T(128)S(1)}, u32[32]{0:T(128)}, u32[]{:S(2)}) copy-start(u32[32]{0:T(128)} %constant.83) | copy-start | bytes 388
  0.6 40.0 %copy-start = (f32[2048]{0:T(1024)S(1)}, f32[2048]{0:T(1024)}, u32[]{:S(2)}) copy-start(f32[2048]{0:T(1024)} %param.10) | copy-start | bytes 24580
  0.7 41.4 %copy-start.1 = (f32[128]{0:T(128)S(1)}, f32[128]{0:T(128)}, u32[]{:S(2)}) copy-start(f32[128]{0:T(128)} %param.8) | copy-start | bytes 1540
  2.5 20.8 %all-to-all-start = ((bf16[128,4,512]{2,0,1:T(8,128)(2,1)}), bf16[128,4,512]{2,0,1:T(8,128)(2,1)S(1)}, u32[]{:S(2)}, u32[]{:S(2)}) async-start(bf16[128,4,512]{2,0,1:T(8,128)(2,1)} %bitcast.46), calls=%async_computation | async-start | bytes 1048576 | tf_op jit(solution)/shard_map/all_to_all | solution.py:32
  23.4 9.1 %collective-permute-start = (bf16[1,512,256]{2,1,0:T(8,128)(2,1)S(1)}, bf16[1,512,256]{2,1,0:T(8,128)(2,1)S(1)}, u32[]{:S(2)}, u32[]{:S(2)}) collective-permute-start(bf16[1,512,256]{2,1,0:T(8,128)(2,1)S(1)} %dynamic-slice_bitcast_fusion), channel_id=1, source_target_pairs={{0,4},{4,8},{8,12},{12,0},{1,5},{5,9},{9,13},{13,1},{2,6},{6,10},{... | collective-permute-start | bytes 786440 | tf_op jit(solution)/shard_map/ppermute | solution.py:48
  32.5 8.2 %collective-permute-start.1 = (bf16[1,512,256]{2,1,0:T(8,128)(2,1)S(1)}, bf16[1,512,256]{2,1,0:T(8,128)(2,1)S(1)}, u32[]{:S(2)}, u32[]{:S(2)}) collective-permute-start(bf16[1,512,256]{2,1,0:T(8,128)(2,1)S(1)} %collective-permute-done), channel_id=1, source_target_pairs={{0,4},{4,8},{8,12},{12,0},{1,5},{5,9},{9,13},{13,1},{2,6},{6,10},{... | collective-permute-start | bytes 786440 | tf_op jit(solution)/shard_map/ppermute | solution.py:48
  40.7 14.2 %collective-permute-start.2 = (bf16[1,512,256]{2,1,0:T(8,128)(2,1)S(1)}, bf16[1,512,256]{2,1,0:T(8,128)(2,1)S(1)}, u32[]{:S(2)}, u32[]{:S(2)}) collective-permute-start(bf16[1,512,256]{2,1,0:T(8,128)(2,1)S(1)} %collective-permute-done.1), channel_id=1, source_target_pairs={{0,4},{4,8},{8,12},{12,0},{1,5},{5,9},{9,13},{13,1},{2,6},{6,10},{... | collective-permute-start | bytes 786440 | tf_op jit(solution)/shard_map/ppermute | solution.py:48
  76.6 8.2 %copy-start.2 = (f32[128]{0:T(128)S(1)}, f32[128]{0:T(128)}, u32[]{:S(2)}) copy-start(f32[128]{0:T(128)} %param.9) | copy-start | bytes 1540
